TPU v7x, 512 devices: a whole 4x4x16 slice. The times are simulated.
512 devices in a mesh: stn: 64 (over x, z_lo, y), chan: 8 (over z_hi, core).
Axes of the slice: x: 4, y: 4, z: 16 (z_hi: 4, z_lo: 4; z = z_hi * 4 + z_lo), core: 2. Of those that a mesh axis runs over, the one named last changes fastest.
Arguments:
- voltages: bfloat16 [512, 2, 143, 2048], P(('stn', 'chan')), may hold values from -6 to 6
- flags: float32 [256, 128], P('stn'), may hold values from 0 to 1, as said below
- station_row: int32 [256], P('stn'), may hold values from 0 to 255, each once
Outputs:
- visibility: bfloat16 [2048, 512, 512], P(('stn', 'chan'))
Inputs may be any that keep to these rules, and one draw needn't show every extreme that they name: `flags`: 0 marks a flagged spectrum of a station, 1 a fully usable one; some stations have 0 at all 128 spectra. `station_row`: every row pair is given to exactly one station.
All inputs are finite; a program needn't handle non-finite values.
Results may differ from a plain program's by a relative error of at most 0.006.
Values may be sent and summed in bfloat16 or wider, within the bound.
No kernel may reach another device: no remote copies, remote signals or barrier semaphores. Data moves between devices by JAX's collectives and lax.ppermute only.
A program may use at most 64 MiB of HBM per device.

v0:
```python
import math
import jax
import jax.numpy as jnp
from jax import lax
from jax.sharding import PartitionSpec as P


def filter_table(taps, lanes):
    total = taps * lanes
    places = jnp.arange(total, dtype=jnp.float32) + 0.5
    window = 0.5 - 0.5 * jnp.cos(2.0 * math.pi * places / total)
    return (jnp.sinc((places - 0.5 * total) / lanes) * window).reshape(taps, lanes)


def dft_tables(length):
    places = jnp.arange(length, dtype=jnp.int32)
    product = places[:, None] * places[None, :] % length
    angle = 2.0 * math.pi * product.astype(jnp.float32) / length
    return (jnp.cos(angle), jnp.sin(angle))


def twiddle_tables(outer, inner):
    product = (
        jnp.arange(outer, dtype=jnp.int32)[:, None]
        * jnp.arange(inner, dtype=jnp.int32)[None, :]
        % (outer * inner)
    )
    angle = 2.0 * math.pi * product.astype(jnp.float32) / (outer * inner)
    return (jnp.cos(angle), jnp.sin(angle))


def contract(form, left, right):
    return jnp.einsum(form, left, right, precision=lax.Precision.HIGHEST)


def channelize(voltages, spectra_count):
    inputs_here = voltages.shape[0]
    lanes = voltages.shape[3]
    taps = voltages.shape[2] - spectra_count + 1
    taps_table = filter_table(taps, lanes)
    real_acc = taps_table[0] * voltages[:, 0, 0:spectra_count, :].astype(jnp.float32)
    imag_acc = taps_table[0] * voltages[:, 1, 0:spectra_count, :].astype(jnp.float32)
    for tap_index in range(1, taps):
        real_acc = real_acc + taps_table[tap_index] * voltages[
            :, 0, tap_index : tap_index + spectra_count, :
        ].astype(jnp.float32)
        imag_acc = imag_acc + taps_table[tap_index] * voltages[
            :, 1, tap_index : tap_index + spectra_count, :
        ].astype(jnp.float32)
    inner = 128
    outer = lanes // inner
    real_grid = real_acc.reshape(inputs_here, spectra_count, outer, inner)
    imag_grid = imag_acc.reshape(inputs_here, spectra_count, outer, inner)
    cos_outer, sin_outer = dft_tables(outer)
    real_mid = contract("gtmn,mk->gtkn", real_grid, cos_outer) + contract(
        "gtmn,mk->gtkn", imag_grid, sin_outer
    )
    imag_mid = contract("gtmn,mk->gtkn", imag_grid, cos_outer) - contract(
        "gtmn,mk->gtkn", real_grid, sin_outer
    )
    cos_twist, sin_twist = twiddle_tables(outer, inner)
    real_twisted = real_mid * cos_twist + imag_mid * sin_twist
    imag_twisted = imag_mid * cos_twist - real_mid * sin_twist
    cos_inner, sin_inner = dft_tables(inner)
    real_out = contract("gtkn,nj->jkgt", real_twisted, cos_inner) + contract(
        "gtkn,nj->jkgt", imag_twisted, sin_inner
    )
    imag_out = contract("gtkn,nj->jkgt", imag_twisted, cos_inner) - contract(
        "gtkn,nj->jkgt", real_twisted, sin_inner
    )
    scale = 1.0 / math.sqrt(lanes)
    stacked = (jnp.stack([real_out, imag_out], axis=3) * scale).astype(jnp.bfloat16)
    return stacked.reshape(lanes, inputs_here, 2 * spectra_count)


def square_products(plain, turned):
    real_part = jnp.einsum("cat,cbt->cab", plain, plain, preferred_element_type=jnp.float32)
    imag_part = jnp.einsum("cat,cbt->cab", plain, turned, preferred_element_type=jnp.float32)
    return (real_part, imag_part)


def on_device(voltages, flags, station_row):
    spectra_count = flags.shape[1]
    inputs_here = voltages.shape[0]
    lanes = voltages.shape[3]
    stn_count = lax.axis_size("stn")
    chan_count = lax.axis_size("chan")
    per_device = lanes // (stn_count * chan_count)
    total_inputs = inputs_here * stn_count * chan_count
    flags_all, rows_all = (
        lax.all_gather(flags, "stn", axis=0, tiled=True),
        lax.all_gather(station_row, "stn", axis=0, tiled=True),
    )
    spectra = channelize(voltages, spectra_count)
    grouped = spectra.reshape(stn_count, chan_count, per_device, inputs_here, 2 * spectra_count)
    order = jnp.argsort(rows_all)
    rows = jnp.arange(total_inputs, dtype=jnp.int32)
    station_of = order[rows // 2]
    source = 2 * station_of + rows % 2
    moved = lax.all_to_all(
        lax.all_to_all(grouped, "stn", split_axis=0, concat_axis=3, tiled=True),
        "chan",
        split_axis=1,
        concat_axis=3,
        tiled=True,
    )
    from_stn = source // (chan_count * inputs_here)
    from_chan = source // inputs_here % chan_count
    within = source % inputs_here
    placed = from_chan * (stn_count * inputs_here) + from_stn * inputs_here + within
    arrived = moved.reshape(per_device, total_inputs, 2, spectra_count)
    weights = jnp.take(flags_all, station_of, axis=0)
    kept = (
        jnp.take(arrived, placed, axis=1).astype(jnp.float32) * weights[None, :, None, :]
    ).astype(jnp.bfloat16)
    plain = kept.reshape(per_device, total_inputs, 2 * spectra_count)
    turned = jnp.concatenate([-kept[:, :, 1], kept[:, :, 0]], axis=-1)
    count = jnp.dot(
        weights, weights.T, preferred_element_type=jnp.float32, precision=lax.Precision.HIGHEST
    )
    denom = jnp.maximum(count, 1.0)
    real_part, imag_part = square_products(plain, turned)
    below = rows[:, None] >= rows[None, :]
    return jnp.where(below[None], real_part / denom, imag_part / denom).astype(jnp.bfloat16)


def solution(mesh):
    placed = (P(("stn", "chan"), None, None, None), P("stn", None), P("stn"))
    return jax.shard_map(
        on_device,
        mesh=mesh,
        in_specs=placed,
        out_specs=P(("stn", "chan"), None, None),
        check_vma=False,
    )
```

profile of v0, /device:TPU:128, one launch (start us, length us, event | category | flops | bytes accessed | tf_op | source)
XLA Modules:
  0.0 374.9 jit_solution(11308704280490452566)
XLA Ops:
  0.0 0.6 fusion.19
  0.6 0.0 copy-start
  0.7 28.6 %slice_convert_fusion.15 = (f32[1,1,128,2048]{3,1,2,0:T(1,128)S(1)}, f32[1,1,128,2048]{3,1,2,0:T(1,128)S(1)}, f32[1,1,128,2048]{3,1,2,0:T(1,128)S(1)}, f32[1,1,1...) fusion(bf16[1,2,143,2048]{3,1,2,0:T(2,128)(2,1)} %param.3), kind=kLoop, calls=%fused_computation.41 | loop fusion | flops 4980736 | bytes 29884416 | tf_op jit(solution)/shard_map/convert_element_type | solution.py:42
  29.3 0.0 copy-done
  29.3 13.9 %slice_convert_fusion.1 = (f32[1,1,128,2048]{3,1,2,0:T(1,128)}, f32[1,1,128,2048]{3,1,2,0:T(1,128)}, f32[1,1,128,2048]{3,1,2,0:T(1,128)}, f32[1,1,128,2048]{3,1,...) fusion(bf16[1,2,143,2048]{3,1,2,0:T(2,128)(2,1)S(1)} %copy-done), kind=kLoop, calls=%fused_computation.27 | loop fusion | flops 3407872 | bytes 20447232 | tf_op jit(solution)/shard_map/convert_element_type | solution.py:49
  43.2 0.7 fusion.62
  43.9 0.7 fusion.114
  44.5 3.2 multiply_add_fusion
  47.7 0.0 copy-start.1
  47.7 0.0 copy-start.2
  47.8 0.0 copy-start.4
  47.8 0.0 copy-start.5
  47.8 0.0 copy-start.6
  47.8 0.0 copy-start.7
  47.8 0.0 copy-start.8
  47.8 0.0 copy-start.9
  47.8 0.0 copy-start.10
  47.8 1.0 fusion.52
  48.9 0.1 copy-done.1
  49.0 0.3 copy-done.2
  49.3 0.0 copy-done.4
  49.3 0.0 copy-done.5
  49.3 0.0 copy-done.6
  49.3 0.0 copy-done.7
  49.3 5.6 %multiply_add_fusion.1 = f32[128,16,128]{2,1,0:T(8,128)S(1)} fusion(f32[128,16,128]{2,1,0:T(8,128)S(1)} %bitcast.127, f32[128,16,128]{2,1,0:T(8,128)S(1)} %bitcast.128, f32[128,16,128]{2,1,0:T(8,128)S(1)} %bitcast.129, f32[128,16,128]{2,1,0:T(8,128)S(1)} %bitcast.130, f32[128,16,128]{2,1,0:T(8,128)S(1)} %bitcast.131, f32[128,16,128]{2,1,0:T(8,128)S(1)} %bitcast.149, ...), kind=kLoop, calls=%fused_computation.42 | loop fusion | flops 8126464 | bytes 17956864 | tf_op jit(solution)/shard_map/add | solution.py:44
  54.9 1.0 fusion.54
  56.0 0.0 copy-start.11
  56.0 0.0 copy-start.12
  56.0 1.1 fusion.3
  57.1 1.3 add_bitcast_fusion
  58.4 1.4 fusion.12
  59.9 1.4 fusion.8
  61.3 1.5 fusion.2
  62.8 1.7 fusion.1
  64.5 0.3 fusion
  64.8 1.1 copy.26
  65.9 0.7 convert_element_type.489
  66.6 41.1 %all_to_all.33 = bf16[64,8,4,1,256]{4,2,1,3,0:T(4,128)(2,1)S(1)} all-to-all(bf16[64,8,4,1,256]{4,2,1,3,0:T(4,128)(2,1)S(1)} %bitcast.147), channel_id=1, replica_groups=mesh['stn'=64,'chan'=8] {'stn'}, dimensions={0} | all-to-all | bytes 2097152 | tf_op jit(solution)/shard_map/all_to_all | solution.py:101
  107.8 0.2 copy.54
  108.0 0.0 copy-start.14
  108.0 1.4 copy.29
  109.4 11.3 %all-to-all-start.1 = ((bf16[1,8,4,64,256]{4,2,3,0,1:T(4,128)(2,1)}), bf16[1,8,4,64,256]{4,2,3,0,1:T(4,128)(2,1)S(1)}, u32[]{:S(2)}, u32[]{:S(2)}) async-start(bf16[1,8,4,64,256]{4,2,3,0,1:T(4,128)(2,1)} %copy.29), calls=%async_computation.1 | async-start | bytes 2097152 | tf_op jit(solution)/shard_map/all_to_all | solution.py:100
  120.6 1.3 dynamic-slice
  122.6 0.2 dynamic-update-slice
  122.8 40.8 %all-reduce = s32[256]{0:T(256)S(1)} all-reduce(s32[256]{0:T(256)S(1)} %dynamic-update-slice), channel_id=1, replica_groups=mesh['stn'=64,'chan'=8] {'stn'}, use_global_device_ids=true, to_apply=%add | all-reduce | flops 256 | bytes 2048
  163.6 3.1 sort.17
  166.8 3.5 gather_fusion
  170.3 192.1 %all-gather = f32[64,4,128]{2,1,0:T(4,128)S(1)} all-gather(f32[1,4,128]{2,1,0:T(4,128)S(1)} %bitcast.167), channel_id=1, replica_groups=mesh['stn'=64,'chan'=8] {'stn'}, dimensions={0}, use_global_device_ids=true | all-gather | bytes 133120 | tf_op jit(solution)/shard_map/all_gather | solution.py:91
  362.4 1.0 gather_fusion.2
  363.5 0.1 broadcast_select_fusion
  363.6 0.1 copy.34
  363.8 0.1 iota_compare_fusion
  363.9 2.0 convolution_maximum_fusion
  365.8 0.0 all-to-all-done.1
  365.8 2.6 gather_fusion.1
  368.5 1.0 copy.43
  369.4 0.3 multiply_convert_fusion
  369.8 0.1 mul.1704
  369.8 0.3 multiply_convert_fusion.1
  370.2 0.8 fusion.117
  371.0 0.0 copy-start.3
  371.0 0.1 fusion.14
  371.1 1.1 copy-done.3
  372.2 2.8 select_convert_fusion
  (16 shorter events, 0.1 us)
Async XLA Ops:
  0.6 28.7 %copy-start = (bf16[1,2,143,2048]{3,1,2,0:T(2,128)(2,1)S(1)}, bf16[1,2,143,2048]{3,1,2,0:T(2,128)(2,1)}, u32[]{:S(2)}) copy-start(bf16[1,2,143,2048]{3,1,2,0:T(2,128)(2,1)} %param.3) | copy-start | bytes 3514372
  47.7 1.2 copy-start.1
  47.7 1.5 copy-start.2
  47.8 1.5 copy-start.4
  47.8 1.5 copy-start.5
  47.8 1.5 copy-start.6
  47.8 1.5 copy-start.7
  47.8 1.5 copy-start.8
  47.8 1.5 copy-start.9
  47.8 1.5 copy-start.10
  56.0 1.1 copy-start.11
  56.0 1.1 copy-start.12
  108.0 14.6 %copy-start.14 = (s32[4]{0:T(128)S(1)}, s32[4]{0:T(128)}, u32[]{:S(2)}) copy-start(s32[4]{0:T(128)} %param.5) | copy-start | bytes 52
  109.4 60.9 %copy-start.13 = (f32[4,128]{1,0:T(4,128)S(1)}, f32[4,128]{1,0:T(4,128)}, u32[]{:S(2)}) copy-start(f32[4,128]{1,0:T(4,128)} %param.4) | copy-start | bytes 6148
  109.4 256.5 %all-to-all-start.1 = ((bf16[1,8,4,64,256]{4,2,3,0,1:T(4,128)(2,1)}), bf16[1,8,4,64,256]{4,2,3,0,1:T(4,128)(2,1)S(1)}, u32[]{:S(2)}, u32[]{:S(2)}) async-start(bf16[1,8,4,64,256]{4,2,3,0,1:T(4,128)(2,1)} %copy.29), calls=%async_computation.1 | async-start | bytes 2097152 | tf_op jit(solution)/shard_map/all_to_all | solution.py:100
  371.0 1.2 copy-start.3
where the time goes:
time: 375 us
  blocking collectives  274 us (73%)
  other arithmetic  57.2 us (15%)
  matrix products  16 us (4%)
  local copies, waits for them, and re-layouts  15.4 us (4%)
  starting transfers between devices  11.3 us (3%)
    all_gather x1, blocking collectives, on_device(): lax.all_gather(flags, 'stn', axis=0, tiled=True)  192 us
    all_to_all x1, blocking collectives, on_device(): lax.all_to_all(grouped, 'stn', split_axis=0, concat_axis=3, tiled=True)  41.1 us
    unnamed x1, blocking collectives  40.8 us
    convert_element_type x1, other arithmetic, channelize(): voltages[:, 1, 0:spectra_count, :].astype(jnp.float32)  28.6 us
    convert_element_type x1, other arithmetic, channelize(): imag_acc = imag_acc + taps_table[tap_index] * voltages[:, 1, tap_index:ta...  13.9 us
    all_to_all x1, starting transfers between devices, on_device(): lax.all_to_all(lax.all_to_all(grouped, 'stn', split_axis=0, concat_axis=3...  11.3 us
    dot_general x8, matrix products, contract(): return jnp.einsum(form, left, right, precision=lax.Precision.HIGHEST)  10.6 us
  transfers between devices with their start and end apart: 1, of which 0 were waited for; matrix products, arithmetic and copies ran while one was open for 3% of the time, Pallas kernels for 0%

commit v1 on v0

--- a/solution.py
+++ b/solution.py
@@ -88,7 +88,9 @@
     per_device = lanes // (stn_count * chan_count)
     total_inputs = inputs_here * stn_count * chan_count
     flags_all, rows_all = (
-        lax.all_gather(flags, "stn", axis=0, tiled=True),
+        jnp.concatenate(
+            lax.all_to_all(jnp.stack([flags] * lax.axis_size("stn")), "stn", 0, 0), axis=0
+        ),
         lax.all_gather(station_row, "stn", axis=0, tiled=True),
     )
     spectra = channelize(voltages, spectra_count)

time: 375 us -> 209 us (0.56)
  the two profiles are of different devices: /device:TPU:128 before, /device:TPU:32 now
where the time goes in v1:
time: 209 us
  blocking collectives  89.7 us (43%)
  other arithmetic  57.2 us (27%)
  starting transfers between devices  20.5 us (10%)
  local copies, waits for them, and re-layouts  16.4 us (8%)
  matrix products  16 us (8%)
  waiting for transfers between devices  7.94 us (4%)
    unnamed x1, blocking collectives  52 us
    all_to_all x1, blocking collectives, on_device(): lax.all_to_all(grouped, 'stn', split_axis=0, concat_axis=3, tiled=True)  37.7 us
    convert_element_type x1, other arithmetic, channelize(): voltages[:, 1, 0:spectra_count, :].astype(jnp.float32)  28.6 us
    convert_element_type x1, other arithmetic, channelize(): imag_acc = imag_acc + taps_table[tap_index] * voltages[:, 1, tap_index:ta...  13.9 us
    all_to_all x1, starting transfers between devices, on_device(): lax.all_to_all(lax.all_to_all(grouped, 'stn', split_axis=0, concat_axis=3...  12.4 us
    dot_general x8, matrix products, contract(): return jnp.einsum(form, left, right, precision=lax.Precision.HIGHEST)  10.6 us
    all_to_all x1, starting transfers between devices, on_device(): lax.all_to_all(jnp.stack([flags] * lax.axis_size('stn')), 'stn', 0, 0)  8.08 us
    all_to_all x1, waiting for transfers between devices, on_device(): lax.all_to_all(jnp.stack([flags] * lax.axis_size('stn')), 'stn', 0, 0)  7.93 us
  transfers between devices with their start and end apart: 2, of which 1 were waited for; matrix products, arithmetic and copies ran while one was open for 6% of the time, Pallas kernels for 0%

profile of v1, /device:TPU:32, one launch (start us, length us, event | category | flops | bytes accessed | tf_op | source)
XLA Modules:
  0.0 208.8 jit_solution(8994661895441307875)
XLA Ops:
  0.0 0.6 fusion.19
  0.6 0.0 copy-start
  0.7 28.6 %slice_convert_fusion.15 = (f32[1,1,128,2048]{3,1,2,0:T(1,128)S(1)}, f32[1,1,128,2048]{3,1,2,0:T(1,128)S(1)}, f32[1,1,128,2048]{3,1,2,0:T(1,128)S(1)}, f32[1,1,1...) fusion(bf16[1,2,143,2048]{3,1,2,0:T(2,128)(2,1)} %param.3), kind=kLoop, calls=%fused_computation.41 | loop fusion | flops 4980736 | bytes 29884416 | tf_op jit(solution)/shard_map/convert_element_type | solution.py:42
  29.3 0.0 copy-done
  29.3 13.9 %slice_convert_fusion.1 = (f32[1,1,128,2048]{3,1,2,0:T(1,128)}, f32[1,1,128,2048]{3,1,2,0:T(1,128)}, f32[1,1,128,2048]{3,1,2,0:T(1,128)}, f32[1,1,128,2048]{3,1,...) fusion(bf16[1,2,143,2048]{3,1,2,0:T(2,128)(2,1)S(1)} %copy-done), kind=kLoop, calls=%fused_computation.27 | loop fusion | flops 3407872 | bytes 20447232 | tf_op jit(solution)/shard_map/convert_element_type | solution.py:49
  43.2 0.7 fusion.62
  43.9 0.7 fusion.114
  44.5 3.2 %multiply_add_fusion = f32[128,16,128]{2,1,0:T(8,128)S(1)} fusion(f32[128,16,128]{2,1,0:T(8,128)} %bitcast.160, f32[128,16,128]{2,1,0:T(8,128)} %bitcast.159, f32[128,16,128]{2,1,0:T(8,128)S(1)} %bitcast.132, f32[128,16,128]{2,1,0:T(8,128)S(1)} %bitcast.133, f32[128,16,128]{2,1,0:T(8,128)S(1)} %bitcast.134, f32[128,16,128]{2,1,0:T(8,128)S(1)} %bitcast.135, ...), kind=kLoop, calls=%fused_computation.25 | loop fusion | flops 8126464 | bytes 17956864 | tf_op jit(solution)/shard_map/add | solution.py:47
  47.7 0.0 copy-start.1
  47.7 0.0 copy-start.2
  47.7 0.0 copy-start.4
  47.7 0.0 copy-start.5
  47.8 0.0 copy-start.6
  47.8 0.0 copy-start.7
  47.8 0.0 copy-start.8
  47.8 0.0 copy-start.9
  47.8 1.0 fusion.52
  48.9 0.1 copy-done.1
  48.9 0.3 copy-done.2
  49.3 5.6 %multiply_add_fusion.1 = f32[128,16,128]{2,1,0:T(8,128)S(1)} fusion(f32[128,16,128]{2,1,0:T(8,128)S(1)} %bitcast.126, f32[128,16,128]{2,1,0:T(8,128)S(1)} %bitcast.127, f32[128,16,128]{2,1,0:T(8,128)S(1)} %bitcast.128, f32[128,16,128]{2,1,0:T(8,128)S(1)} %bitcast.129, f32[128,16,128]{2,1,0:T(8,128)S(1)} %bitcast.130, f32[128,16,128]{2,1,0:T(8,128)S(1)} %bitcast.148, ...), kind=kLoop, calls=%fused_computation.42 | loop fusion | flops 8126464 | bytes 17956864 | tf_op jit(solution)/shard_map/add | solution.py:44
  54.9 1.0 fusion.54
  55.9 0.0 copy-start.11
  55.9 0.0 copy-start.12
  56.0 1.1 fusion.3
  57.0 0.0 copy-done.11
  57.1 0.0 copy-done.12
  57.1 1.3 add_bitcast_fusion
  58.4 1.4 fusion.12
  59.8 1.4 fusion.8
  61.3 1.5 fusion.2
  62.8 1.7 fusion.1
  64.5 0.3 fusion
  64.8 1.1 copy.26
  65.9 0.0 copy-start.13
  65.9 0.7 convert_element_type.489
  66.6 37.7 %all_to_all.38 = bf16[64,8,4,1,256]{4,2,1,3,0:T(4,128)(2,1)S(1)} all-to-all(bf16[64,8,4,1,256]{4,2,1,3,0:T(4,128)(2,1)S(1)} %bitcast.146), channel_id=1, replica_groups=mesh['stn'=64,'chan'=8] {'stn'}, dimensions={0} | all-to-all | bytes 2097152 | tf_op jit(solution)/shard_map/all_to_all | solution.py:103
  104.3 0.7 stack.11
  104.9 8.1 %all-to-all-start.2 = ((f32[64,4,128]{2,1,0:T(4,128)}), f32[64,4,128]{2,1,0:T(4,128)S(1)}, u32[]{:S(2)}, u32[]{:S(2)}) async-start(f32[64,4,128]{2,1,0:T(4,128)} %stack.11), calls=%async_computation.2 | async-start | bytes 262144 | tf_op jit(solution)/shard_map/all_to_all | solution.py:92
  113.0 0.2 copy.54
  113.3 0.0 copy-start.14
  113.3 1.4 copy.29
  114.6 7.9 %all-to-all-done.2 = f32[64,4,128]{2,1,0:T(4,128)S(1)} async-done(((f32[64,4,128]{2,1,0:T(4,128)}), f32[64,4,128]{2,1,0:T(4,128)S(1)}, u32[]{:S(2)}, u32[]{:S(2)}) %all-to-all-start.2) | async-done | bytes 131104 | tf_op jit(solution)/shard_map/all_to_all | solution.py:92
  122.6 12.4 %all-to-all-start.1 = ((bf16[1,8,4,64,256]{4,2,3,0,1:T(4,128)(2,1)}), bf16[1,8,4,64,256]{4,2,3,0,1:T(4,128)(2,1)S(1)}, u32[]{:S(2)}, u32[]{:S(2)}) async-start(bf16[1,8,4,64,256]{4,2,3,0,1:T(4,128)(2,1)} %copy.29), calls=%async_computation.1 | async-start | bytes 2097152 | tf_op jit(solution)/shard_map/all_to_all | solution.py:102
  135.0 1.3 dynamic-slice
  136.9 0.2 dynamic-update-slice
  137.2 52.0 %all-reduce = s32[256]{0:T(256)S(1)} all-reduce(s32[256]{0:T(256)S(1)} %dynamic-update-slice), channel_id=1, replica_groups=mesh['stn'=64,'chan'=8] {'stn'}, use_global_device_ids=true, to_apply=%add | all-reduce | flops 256 | bytes 2048
  189.2 3.2 %sort.17 = (s32[256]{0:T(256)}, s32[256]{0:T(256)S(1)}) sort(s32[256]{0:T(256)S(1)} %all-reduce, s32[256]{0:T(256)S(1)} %iota.415), dimensions={0}, to_apply=%region_0.1 | sort | flops 2048 | bytes 4096 | tf_op jit(solution)/shard_map/jit(argsort)/sort | solution.py:98
  192.4 3.8 %gather_fusion = s32[512]{0:T(512)S(1)} fusion(s32[256]{0:T(256)S(1)} %get-tuple-element.6, s32[1024]{0:T(1024)S(1)} %pad_clamp_fusion.2), kind=kCustom, calls=%fused_computation | custom fusion | bytes 6144 | tf_op jit(solution)/shard_map/gather | solution.py:100
  196.2 0.1 iota_compare_fusion
  196.4 1.0 gather_fusion.2
  197.4 0.1 broadcast_select_fusion
  197.5 0.1 copy.34
  197.7 2.0 convolution_maximum_fusion
  199.6 0.0 all-to-all-done.1
  199.6 2.6 %gather_fusion.1 = bf16[512,4,2,128]{3,1,2,0:T(4,128)(2,1)S(1)} fusion(bf16[4,512,2,128]{3,0,2,1:T(4,128)(2,1)S(1)} %bitcast.145, s32[1024]{0:T(1024)S(1)} %pad_clamp_fusion.1), kind=kCustom, calls=%fused_computation.1 | custom fusion | bytes 2099200 | tf_op jit(solution)/shard_map/jit(_take)/gather | solution.py:116
  202.3 1.0 copy.43
  203.2 0.3 multiply_convert_fusion
  203.6 0.1 mul.1704
  203.7 0.3 multiply_convert_fusion.1
  204.0 0.8 fusion.117
  204.8 0.0 copy-start.3
  204.8 0.1 fusion.14
  204.9 1.1 copy-done.3
  206.0 2.8 %select_convert_fusion = bf16[4,512,512]{2,1,0:T(8,128)(2,1)} fusion(f32[4,512,512]{2,1,0:T(8,128)S(1)} %fusion.117, f32[512,512]{1,0:T(8,128)S(1)} %copy-done.3, pred[512,512]{1,0:T(8,128)(4,1)S(1)} %iota_compare_fusion, bf16[4,512,256]{1,2,0:T(8,128)(2,1)S(1)} %multiply_convert_fusion.1, bf16[4,512,128]{2,1,0:T(8,128)(2,1)S(1)} %get-tuple-element.42, ...), kind=kOutput, calls=%fused_computation.3 | convolution fusion | flops 543162368 | bytes 9699328 | tf_op jit(solution)/shard_map/cat,cbt->cab/dot_general | solution.py:78
  (18 shorter events, 0.1 us)
Async XLA Ops:
  0.6 28.7 %copy-start = (bf16[1,2,143,2048]{3,1,2,0:T(2,128)(2,1)S(1)}, bf16[1,2,143,2048]{3,1,2,0:T(2,128)(2,1)}, u32[]{:S(2)}) copy-start(bf16[1,2,143,2048]{3,1,2,0:T(2,128)(2,1)} %param.3) | copy-start | bytes 3514372
  47.7 1.2 copy-start.1
  47.7 1.5 copy-start.2
  47.7 1.5 copy-start.4
  47.7 1.5 copy-start.5
  47.8 1.5 copy-start.6
  47.8 1.5 copy-start.7
  47.8 1.5 copy-start.8
  47.8 1.5 copy-start.9
  47.8 1.5 copy-start.10
  55.9 1.1 copy-start.11
  55.9 1.1 copy-start.12
  65.9 38.4 %copy-start.13 = (f32[4,128]{1,0:T(4,128)S(1)}, f32[4,128]{1,0:T(4,128)}, u32[]{:S(2)}) copy-start(f32[4,128]{1,0:T(4,128)} %param.4) | copy-start | bytes 6148
  104.9 17.6 %all-to-all-start.2 = ((f32[64,4,128]{2,1,0:T(4,128)}), f32[64,4,128]{2,1,0:T(4,128)S(1)}, u32[]{:S(2)}, u32[]{:S(2)}) async-start(f32[64,4,128]{2,1,0:T(4,128)} %stack.11), calls=%async_computation.2 | async-start | bytes 262144 | tf_op jit(solution)/shard_map/all_to_all | solution.py:92
  113.3 23.7 %copy-start.14 = (s32[4]{0:T(128)S(1)}, s32[4]{0:T(128)}, u32[]{:S(2)}) copy-start(s32[4]{0:T(128)} %param.5) | copy-start | bytes 52
  122.6 77.1 %all-to-all-start.1 = ((bf16[1,8,4,64,256]{4,2,3,0,1:T(4,128)(2,1)}), bf16[1,8,4,64,256]{4,2,3,0,1:T(4,128)(2,1)S(1)}, u32[]{:S(2)}, u32[]{:S(2)}) async-start(bf16[1,8,4,64,256]{4,2,3,0,1:T(4,128)(2,1)} %copy.29), calls=%async_computation.1 | async-start | bytes 2097152 | tf_op jit(solution)/shard_map/all_to_all | solution.py:102
  204.8 1.2 copy-start.3
